TPU v7x, 32 devices: a whole 2x2x4 slice. The times are simulated.
32 devices in a mesh: seq: 8 (over y, x, core), red: 4 (over z).
Axes of the slice: x: 2, y: 2, z: 4, core: 2. Of those that a mesh axis runs over, the one named last changes fastest.
Arguments:
- token_ids: int32 [1024], P('seq'), may hold values from 0 to 511
- embedding: bfloat16 [512, 4096], P(None, 'red'), may hold values from -6 to 6
- proj_weight: bfloat16 [4096, 3, 4, 256], P('red', None, None, 'seq'), may hold values from -0.09375 to 0.09375
- filters: float32 [1024, 1024], P('seq', 'red'), may hold values from -1 to 1
- cotangent: float32 [1024, 1024], P('seq', 'red'), may hold values from -6 to 6
Outputs:
- output: float32 [1024, 1024], P('seq', 'red')
- filter_grad: float32 [1024, 1024], P('seq', 'red')
- branch_grads: bfloat16 [1024, 3, 1024], P('seq', None, 'red')
- weight_grad: float32 [4096, 3, 4, 256], P('red', None, None, 'seq')
All inputs are finite; a program needn't handle non-finite values.
Results may differ from a plain program's by a relative error of at most 0.0029.
Values sent between devices are 32-bit elements; how exact they have to be, the bound alone decides.
A program may use at most 64 MiB of HBM per device.

v0:
```python
import math
import jax
import jax.numpy as jnp
from jax import lax
from jax.sharding import PartitionSpec as P

precise_mode = lax.Precision.HIGHEST


def angles(numbers, modulus, direction):
    phase = (numbers % modulus).astype(jnp.float32) * (direction * 2.0 * math.pi / modulus)
    return (jnp.cos(phase), jnp.sin(phase))


def rotate(real_part, imag_part, cosine, sine_part):
    return (real_part * cosine - imag_part * sine_part, real_part * sine_part + imag_part * cosine)


def complex_einsum(formula, matrix, values):
    mat_real, mat_imag = matrix
    val_real, val_imag = values
    real_out = jnp.einsum(formula, mat_real, val_real, precision=precise_mode) - jnp.einsum(
        formula, mat_imag, val_imag, precision=precise_mode
    )
    imag_out = jnp.einsum(formula, mat_real, val_imag, precision=precise_mode) + jnp.einsum(
        formula, mat_imag, val_real, precision=precise_mode
    )
    return (real_out, imag_out)


def factors(length_total):
    first_factor = 1
    for candidate in range(1, math.isqrt(length_total) + 1):
        if length_total % candidate == 0:
            first_factor = candidate
    return (first_factor, length_total // first_factor)


def combine_spectra(spec_real, spec_imag, width):
    filt_re = spec_real[..., :width]
    inner_re = spec_real[..., width : 2 * width]
    up_re = spec_real[..., 2 * width :]
    filt_im = spec_imag[..., :width]
    inner_im = spec_imag[..., width : 2 * width]
    up_im = spec_imag[..., 2 * width :]
    joined_real = jnp.concatenate(
        [
            filt_re * inner_re - filt_im * inner_im,
            filt_re * up_re + filt_im * up_im,
            up_re * inner_re + up_im * inner_im,
        ],
        axis=-1,
    )
    joined_imag = jnp.concatenate(
        [
            filt_re * inner_im + filt_im * inner_re,
            filt_re * up_im - filt_im * up_re,
            up_im * inner_re - up_re * inner_im,
        ],
        axis=-1,
    )
    return (joined_real, joined_imag)


def local_convolve(signals):
    length, branch_count, narrow = signals.shape
    total = 2 * length
    first_factor, second_factor = factors(total)
    flat = signals.reshape(length, branch_count * narrow)
    padded = jnp.concatenate([flat, jnp.zeros_like(flat)], axis=0).reshape(
        first_factor, second_factor, branch_count * narrow
    )
    first_index = jnp.arange(first_factor, dtype=jnp.int32)
    second_index = jnp.arange(second_factor, dtype=jnp.int32)
    cosine, sine_part = angles(first_index[:, None] * first_index[None, :], first_factor, -1.0)
    real_part = jnp.einsum("kn,nbm->kbm", cosine, padded, precision=precise_mode)
    imag_part = jnp.einsum("kn,nbm->kbm", sine_part, padded, precision=precise_mode)
    cosine, sine_part = angles(first_index[:, None] * second_index[None, :], total, -1.0)
    real_part, imag_part = rotate(real_part, imag_part, cosine[:, :, None], sine_part[:, :, None])
    real_part, imag_part = complex_einsum(
        "lb,kbm->klm",
        angles(second_index[:, None] * second_index[None, :], second_factor, -1.0),
        (real_part, imag_part),
    )
    real_part, imag_part = combine_spectra(real_part, imag_part, narrow)
    real_part, imag_part = complex_einsum(
        "bl,klm->kbm",
        angles(second_index[:, None] * second_index[None, :], second_factor, 1.0),
        (real_part, imag_part),
    )
    cosine, sine_part = angles(first_index[:, None] * second_index[None, :], total, 1.0)
    real_part, imag_part = rotate(real_part, imag_part, cosine[:, :, None], sine_part[:, :, None])
    cosine, sine_part = angles(first_index[:, None] * first_index[None, :], first_factor, 1.0)
    result = jnp.einsum("nk,kbm->nbm", cosine, real_part, precision=precise_mode) - jnp.einsum(
        "nk,kbm->nbm", sine_part, imag_part, precision=precise_mode
    )
    result = result.reshape(total, branch_count * narrow)[:length] / total
    return result.reshape(length, branch_count, narrow)


def shards(token_ids, embedding, proj_weight, filters, cotangent):
    tok_count = token_ids.shape[0]
    devices = lax.axis_size("seq")
    width = filters.shape[1]
    vocabulary = embedding.shape[0]
    width_rows, branches, red_count, piece = proj_weight.shape
    scale_factor = float(tok_count * devices) ** (-0.5)
    table = jnp.dot(
        embedding,
        proj_weight.reshape(width_rows, branches * red_count * piece),
        preferred_element_type=jnp.float32,
    )
    table = table.reshape(vocabulary, branches, red_count, piece)
    own_table = lax.psum_scatter(table, "red", scatter_dimension=2, tiled=True)
    full_table = lax.all_gather(own_table, "seq", axis=3, tiled=True)
    projected = jnp.take(full_table, token_ids, axis=0)
    projected = projected.reshape(tok_count, branches, width)
    queries = projected[:, 0]
    key_rows = projected[:, 1]
    value_rows = projected[:, 2]
    inner = key_rows * value_rows
    upstream = cotangent * queries
    stacked = jnp.stack([filters, inner, upstream], axis=1)
    whole_length = lax.all_to_all(stacked, "seq", split_axis=2, concat_axis=0, tiled=True)
    results = local_convolve(whole_length)
    returned = lax.all_to_all(results, "seq", split_axis=0, concat_axis=2, tiled=True)
    conv = returned[:, 0]
    grad_inner = returned[:, 1]
    filter_raw = returned[:, 2]
    output = queries * conv
    filter_grad = filter_raw * scale_factor
    branch_grads = jnp.stack(
        [cotangent * conv, grad_inner * value_rows, grad_inner * key_rows], axis=1
    ).astype(jnp.bfloat16)
    one_hot = (token_ids[:, None] == lax.iota(jnp.int32, vocabulary)[None, :]).astype(jnp.bfloat16)
    token_sums = lax.dot_general(
        one_hot,
        branch_grads.reshape(tok_count, branches * width),
        (((0,), (0,)), ((), ())),
        preferred_element_type=jnp.float32,
    )
    summed = lax.psum_scatter(
        token_sums.reshape(vocabulary, branches, width), "seq", scatter_dimension=2, tiled=True
    )
    gathered = lax.all_gather(summed[:, :, None, :], "red", axis=2, tiled=True)
    weight_grad = (
        lax.dot_general(
            embedding.astype(jnp.float32),
            gathered.reshape(vocabulary, branches * red_count * piece),
            (((0,), (0,)), ((), ())),
            precision=precise_mode,
        )
        * scale_factor
    )
    return (
        output,
        filter_grad,
        branch_grads,
        weight_grad.reshape(width_rows, branches, red_count, piece),
    )


def solution(mesh):
    in_specs = (
        P("seq"),
        P(None, "red"),
        P("red", None, None, "seq"),
        P("seq", "red"),
        P("seq", "red"),
    )
    out_specs = (
        P("seq", "red"),
        P("seq", "red"),
        P("seq", None, "red"),
        P("red", None, None, "seq"),
    )
    return jax.shard_map(shards, mesh=mesh, in_specs=in_specs, out_specs=out_specs, check_vma=False)
```

profile of v0, /device:TPU:0, one launch (start us, length us, event | category | flops | bytes accessed | tf_op | source)
XLA Modules:
  0.0 223.0 jit_solution(11435874289733762096)
XLA Ops:
  8.4 2.6 %fusion.2 = f32[512,3,4,32]{0,3,2,1:T(8,128)} fusion(bf16[512,1024]{1,0:T(8,128)(2,1)S(1)} %copy-done, bf16[1024,3,4,32]{0,3,2,1:T(8,128)(2,1)} %param.7), kind=kOutput, calls=%fused_computation.10 | convolution fusion | flops 402653184 | bytes 2621440 | tf_op jit(solution)/shard_map/dot_general | solution.py:108
  11.7 46.1 %all-reduce.4.cloned.1.call-done = f32[512,3,4,32]{0,3,2,1:T(8,128)} async-done(((f32[512,3,4,32]{0,3,2,1:T(8,128)}), f32[512,3,4,32]{0,3,2,1:T(8,128)}) %all-reduce.4.cloned.1.call-update) | async-done | bytes 786448
  57.8 1.6 constant_dynamic-slice_fusion
  60.4 24.8 %all-gather.3.cloned.1.call-done = f32[512,3,1,256]{0,2,1,3:T(1,128)} async-done(((f32[512,3,1,32]{0,2,1,3:T(1,128)}), f32[512,3,1,256]{0,2,1,3:T(1,128)}) %all-gather.3.cloned.1.call-update) | async-done | bytes 1572880 | tf_op jit(solution)/shard_map/all_gather | solution.py:115
  85.2 4.7 %copy.121 = f32[512,3,1,256]{3,1,0,2:T(4,128)S(1)} copy(f32[512,3,1,256]{0,2,1,3:T(1,128)} %all-gather.3.cloned.1.call-done) | data formatting | bytes 3145728 | tf_op jit(solution)/shard_map/all_gather | solution.py:115
  89.9 1.6 gather_fusion
  91.5 1.2 broadcast_select_fusion
  95.9 3.5 %all-to-all-start = ((f32[128,3,256]{0,1,2:T(4,128)}), f32[128,3,256]{0,1,2:T(4,128)S(1)}, u32[]{:S(2)}, u32[]{:S(2)}) async-start(f32[128,3,256]{0,1,2:T(4,128)} %copy.123), calls=%async_computation | async-start | bytes 1048576 | tf_op jit(solution)/shard_map/all_to_all | solution.py:124
  100.0 9.0 %all-to-all-done = f32[128,3,256]{0,1,2:T(4,128)S(1)} async-done(((f32[128,3,256]{0,1,2:T(4,128)}), f32[128,3,256]{0,1,2:T(4,128)S(1)}, u32[]{:S(2)}, u32[]{:S(2)}) %all-to-all-start) | async-done | bytes 393248 | tf_op jit(solution)/shard_map/all_to_all | solution.py:124
  109.7 1.6 fusion.16
  111.3 1.9 multiply_subtract_fusion.3
  113.2 1.7 fusion.12
  115.0 1.7 fusion.8
  116.7 1.8 fusion.1
  118.5 1.8 fusion
  120.4 1.4 multiply_subtract_fusion.2
  122.9 1.6 fusion.34
  124.5 1.6 fusion.32
  126.1 1.6 convolution_add_fusion
  127.7 2.0 subtract_bitcast_fusion
  129.6 1.6 fusion.4
  131.2 1.6 fusion.6
  133.9 2.3 %reshape.135 = f32[1024,3,32]{2,1,0:T(4,128)S(1)} reshape(f32[16,64,96]{2,1,0:T(8,128)} %copy.148) | data formatting | bytes 786432 | tf_op jit(solution)/shard_map/div | solution.py:97
  136.2 1.3 reshape.139
  137.5 10.7 %all_to_all.33 = f32[8,1,12288]{2,1,0:T(1,128)S(1)} all-to-all(f32[8,1,12288]{2,1,0:T(1,128)S(1)} %reshape.139), channel_id=1, replica_groups=mesh['seq'=8,'red'=4] {'seq'}, dimensions={0} | all-to-all | bytes 786432 | tf_op jit(solution)/shard_map/all_to_all | solution.py:126
  148.8 1.6 reduce
  150.3 1.3 reshape.140
  152.5 1.5 slice_multiply_fusion.1
  154.9 1.6 fusion.21
  158.7 35.4 %reduce-scatter.5.cloned.1.call-done = f32[512,3,32]{0,2,1:T(8,128)} async-done(((f32[512,3,256]{0,2,1:T(8,128)}), f32[512,3,32]{0,2,1:T(8,128)}) %reduce-scatter.5.cloned.1.call-update) | async-done | bytes 196624 | tf_op jit(solution)/shard_map/reduce_scatter | solution.py:142
  194.1 19.8 %all-gather = f32[512,3,128]{0,2,1:T(8,128)S(1)} all-gather(f32[512,3,32]{0,2,1:T(8,128)} %reduce-scatter.5.cloned.1.call-done), channel_id=2, replica_groups=mesh['seq'=8,'red'=4] {'red'}, dimensions={2}, use_global_device_ids=true | all-gather | bytes 983040 | tf_op jit(solution)/shard_map/all_gather | solution.py:145
  213.9 2.5 %convolution_multiply_fusion = f32[384,1024]{1,0:T(8,128)} fusion(f32[512,384]{0,1:T(8,128)S(1)} %bitcast.117, bf16[512,1024]{1,0:T(8,128)(2,1)S(1)} %copy-done), kind=kOutput, calls=%fused_computation.1 | convolution fusion | flops 2416312320 | bytes 3407872 | tf_op jit(solution)/shard_map/dot_general | solution.py:147
  (60 shorter events, 13.7 us)
Async XLA Ops:
  7.2 1.2 copy-start
  7.2 3.9 %copy-start.8 = (u32[32]{0:T(128)S(1)}, u32[32]{0:T(128)}, u32[]{:S(2)}) copy-start(u32[32]{0:T(128)} %constant.91) | copy-start | bytes 388
  7.2 50.6 %all-reduce.4.cloned.1.call-start = ((), (), s32[]{:S(2)}) async-start(), calls=%async_computation.5 | async-start | bytes 1572864
  11.0 49.2 %copy-start.6 = (f32[128,256]{1,0:T(8,128)S(1)}, f32[128,256]{1,0:T(8,128)}, u32[]{:S(2)}) copy-start(f32[128,256]{1,0:T(8,128)} %param.8) | copy-start | bytes 393220
  11.0 49.4 %copy-start.7 = (s32[128]{0:T(128)S(1)}, s32[128]{0:T(128)}, u32[]{:S(2)}) copy-start(s32[128]{0:T(128)} %param.5) | copy-start | bytes 1540
  11.0 74.2 %all-gather.3.cloned.1.call-start = ((), (), s32[]{:S(2)}) async-start(), calls=%async_computation.3 | async-start | bytes 1769472 | tf_op jit(solution)/shard_map/all_gather | solution.py:115
  89.9 4.0 %copy-start.4 = (f32[128,256]{1,0:T(8,128)S(1)}, f32[128,256]{1,0:T(8,128)}, u32[]{:S(2)}) copy-start(f32[128,256]{1,0:T(8,128)} %param.9) | copy-start | bytes 393220
  92.8 0.8 copy-start.1
  93.8 0.7 copy-start.2
  95.9 13.2 %all-to-all-start = ((f32[128,3,256]{0,1,2:T(4,128)}), f32[128,3,256]{0,1,2:T(4,128)S(1)}, u32[]{:S(2)}, u32[]{:S(2)}) async-start(f32[128,3,256]{0,1,2:T(4,128)} %copy.123), calls=%async_computation | async-start | bytes 1048576 | tf_op jit(solution)/shard_map/all_to_all | solution.py:124
  99.4 94.7 %reduce-scatter.5.cloned.1.call-start = ((), (), s32[]{:S(2)}) async-start(), calls=%async_computation.4 | async-start | bytes 1769472 | tf_op jit(solution)/shard_map/reduce_scatter | solution.py:142
  152.3 1.8 copy-start.5
  156.5 1.5 copy-start.3
Sparse Core Ops, SparseCore 0:
  11.2 46.5 all-reduce.3
  60.4 24.8 all-gather.2
  156.7 37.3 reduce-scatter.4
where the time goes:
time: 224 us; the launch traced here: 223 us
  waiting for transfers between devices  115 us (51%)
  blocking collectives  30.5 us (14%)
  matrix products  27.3 us (12%)
  local copies, waits for them, and re-layouts  22.8 us (10%)
  between operations  14.2 us (6%)
  other arithmetic  9.04 us (4%)
  starting transfers between devices  3.8 us (2%)
    unnamed x4, waiting for transfers between devices  46.1 us
    reduce_scatter x1, waiting for transfers between devices, shards(): lax.psum_scatter(token_sums.reshape(vocabulary, branches, width), 'seq',...  35.4 us
    all_gather x1, waiting for transfers between devices, shards(): full_table = lax.all_gather(own_table, 'seq', axis=3, tiled=True)  24.8 us
    all_gather x1, blocking collectives, shards(): gathered = lax.all_gather(summed[:, :, None, :], 'red', axis=2, tiled=True)  19.8 us
    all_to_all x1, blocking collectives, shards(): lax.all_to_all(results, 'seq', split_axis=0, concat_axis=2, tiled=True)  10.7 us
    unnamed x28, local copies, waits for them, and re-layouts  9.24 us
    all_to_all x1, waiting for transfers between devices, shards(): lax.all_to_all(stacked, 'seq', split_axis=2, concat_axis=0, tiled=True)  8.98 us
    all_gather x1, local copies, waits for them, and re-layouts, shards(): full_table = lax.all_gather(own_table, 'seq', axis=3, tiled=True)  4.65 us
  transfers between devices with their start and end apart: 4, of which 4 were waited for; matrix products, arithmetic and copies ran while one was open for 1% of the time, Pallas kernels for 0%

commit v1 on v0

--- a/solution.py
+++ b/solution.py
@@ -123,7 +123,16 @@
     stacked = jnp.stack([filters, inner, upstream], axis=1)
     whole_length = lax.all_to_all(stacked, "seq", split_axis=2, concat_axis=0, tiled=True)
     results = local_convolve(whole_length)
-    returned = lax.all_to_all(results, "seq", split_axis=0, concat_axis=2, tiled=True)
+
+    def bring_pipes(unit):
+        near = jax.lax.psum(1, "seq")
+        long_array = jnp.split(unit, near, axis=0)
+        b_next = jnp.stack(long_array, axis=0)
+        return jnp.concatenate(
+            jax.lax.all_to_all(b_next, "seq", split_axis=0, concat_axis=0), axis=2
+        )
+
+    returned = bring_pipes(results)
     conv = returned[:, 0]
     grad_inner = returned[:, 1]
     filter_raw = returned[:, 2]

time: 224 us -> 215 us (0.960)
  local copies, waits for them, and re-layouts: 22.8 us -> 16.7 us
  other arithmetic: 9.04 us -> 6.25 us
    unnamed x28 -> x25, local copies, waits for them, and re-layouts: 9.24 us -> 5.33 us
    div x2 -> x0, local copies, waits for them, and re-layouts: 3.26 us -> none  [local_convolve(): result = result.reshape(total, branch_count * narrow)[:length] / total]
  transfers between devices with their start and end apart: 4 -> 4, of which waited for: 4 -> 4; matrix products, arithmetic and copies ran while one was open for 1% -> 2% of each run, Pallas kernels for 0% -> 0%
where the time goes in v1:
time: 215 us; the launch traced here: 214 us
  waiting for transfers between devices  115 us (53%)
  blocking collectives  30.4 us (14%)
  matrix products  27.3 us (13%)
  local copies, waits for them, and re-layouts  16.7 us (8%)
  between operations  14.2 us (7%)
  other arithmetic  6.25 us (3%)
  starting transfers between devices  3.8 us (2%)
    unnamed x4, waiting for transfers between devices  46.1 us
    reduce_scatter x1, waiting for transfers between devices, shards(): lax.psum_scatter(token_sums.reshape(vocabulary, branches, width), 'seq',...  35.4 us
    all_gather x1, waiting for transfers between devices, shards(): full_table = lax.all_gather(own_table, 'seq', axis=3, tiled=True)  24.8 us
    all_gather x1, blocking collectives, shards(): gathered = lax.all_gather(summed[:, :, None, :], 'red', axis=2, tiled=True)  19.7 us
    all_to_all x1, blocking collectives, bring_pipes(): jax.lax.all_to_all(b_next, 'seq', split_axis=0, concat_axis=0)  10.7 us
    all_to_all x1, waiting for transfers between devices, shards(): lax.all_to_all(stacked, 'seq', split_axis=2, concat_axis=0, tiled=True)  8.98 us
    unnamed x25, local copies, waits for them, and re-layouts  5.33 us
    all_gather x1, local copies, waits for them, and re-layouts, shards(): full_table = lax.all_gather(own_table, 'seq', axis=3, tiled=True)  4.65 us
  transfers between devices with their start and end apart: 4, of which 4 were waited for; matrix products, arithmetic and copies ran while one was open for 2% of the time, Pallas kernels for 0%

profile of v1, /device:TPU:0, one launch (start us, length us, event | category | flops | bytes accessed | tf_op | source)
XLA Modules:
  0.0 214.1 jit_solution(14623932902881521271)
XLA Ops:
  7.2 1.2 copy-done
  8.4 2.6 %fusion.2 = f32[512,3,4,32]{0,3,2,1:T(8,128)} fusion(bf16[512,1024]{1,0:T(8,128)(2,1)S(1)} %copy-done, bf16[1024,3,4,32]{0,3,2,1:T(8,128)(2,1)} %param.7), kind=kOutput, calls=%fused_computation.10 | convolution fusion | flops 402653184 | bytes 2621440 | tf_op jit(solution)/shard_map/dot_general | solution.py:108
  11.7 46.1 %all-reduce.4.cloned.1.call-done = f32[512,3,4,32]{0,3,2,1:T(8,128)} async-done(((f32[512,3,4,32]{0,3,2,1:T(8,128)}), f32[512,3,4,32]{0,3,2,1:T(8,128)}) %all-reduce.4.cloned.1.call-update) | async-done | bytes 786448
  57.8 1.6 constant_dynamic-slice_fusion
  59.4 0.9 copy.144
  60.4 24.8 %all-gather.3.cloned.1.call-done = f32[512,3,1,256]{0,2,1,3:T(1,128)} async-done(((f32[512,3,1,32]{0,2,1,3:T(1,128)}), f32[512,3,1,256]{0,2,1,3:T(1,128)}) %all-gather.3.cloned.1.call-update) | async-done | bytes 1572880 | tf_op jit(solution)/shard_map/all_gather | solution.py:115
  85.2 4.7 %copy.145 = f32[512,3,1,256]{3,1,0,2:T(4,128)S(1)} copy(f32[512,3,1,256]{0,2,1,3:T(1,128)} %all-gather.3.cloned.1.call-done) | data formatting | bytes 3145728 | tf_op jit(solution)/shard_map/all_gather | solution.py:115
  89.9 1.6 gather_fusion
  91.5 1.2 broadcast_select_fusion
  93.5 1.0 copy.147
  94.6 3.5 %all-to-all-start = ((f32[128,3,256]{0,1,2:T(4,128)}), f32[128,3,256]{0,1,2:T(4,128)S(1)}, u32[]{:S(2)}, u32[]{:S(2)}) async-start(f32[128,3,256]{0,1,2:T(4,128)} %copy.147), calls=%async_computation | async-start | bytes 1048576 | tf_op jit(solution)/shard_map/all_to_all | solution.py:124
  98.7 9.0 %all-to-all-done = f32[128,3,256]{0,1,2:T(4,128)S(1)} async-done(((f32[128,3,256]{0,1,2:T(4,128)}), f32[128,3,256]{0,1,2:T(4,128)S(1)}, u32[]{:S(2)}, u32[]{:S(2)}) %all-to-all-start) | async-done | bytes 393248 | tf_op jit(solution)/shard_map/all_to_all | solution.py:124
  108.3 1.6 fusion.16
  109.9 1.9 multiply_subtract_fusion.3
  111.9 1.7 fusion.12
  113.7 1.7 fusion.8
  115.4 1.8 fusion.1
  117.2 1.8 fusion
  119.0 1.4 multiply_subtract_fusion.2
  120.4 1.1 multiply_add_fusion.2
  121.6 1.6 fusion.34
  123.2 1.6 fusion.32
  124.8 1.6 convolution_add_fusion
  126.4 2.0 subtract_bitcast_fusion
  128.3 1.6 fusion.4
  129.9 1.6 fusion.6
  134.0 10.7 %all_to_all.20 = f32[8,128,3,32]{1,3,2,0:T(8,128)S(1)} all-to-all(f32[8,128,3,32]{1,3,2,0:T(8,128)S(1)} %constant_dynamic-update-slice_fusion), channel_id=1, replica_groups=mesh['seq'=8,'red'=4] {'seq'}, dimensions={0} | all-to-all | bytes 786432 | tf_op jit(solution)/shard_map/all_to_all | solution.py:132
  146.1 1.6 fusion.21
  148.4 0.8 copy.174
  149.9 35.4 %reduce-scatter.5.cloned.1.call-done = f32[512,3,32]{0,2,1:T(8,128)} async-done(((f32[512,3,256]{0,2,1:T(8,128)}), f32[512,3,32]{0,2,1:T(8,128)}) %reduce-scatter.5.cloned.1.call-update) | async-done | bytes 196624 | tf_op jit(solution)/shard_map/reduce_scatter | solution.py:151
  185.3 19.7 %all-gather = f32[512,3,128]{0,2,1:T(8,128)S(1)} all-gather(f32[512,3,32]{0,2,1:T(8,128)} %reduce-scatter.5.cloned.1.call-done), channel_id=2, replica_groups=mesh['seq'=8,'red'=4] {'red'}, dimensions={2}, use_global_device_ids=true | all-gather | bytes 983040 | tf_op jit(solution)/shard_map/all_gather | solution.py:154
  205.0 2.5 %convolution_multiply_fusion = f32[384,1024]{1,0:T(8,128)} fusion(f32[512,384]{0,1:T(8,128)S(1)} %bitcast.129, bf16[512,1024]{1,0:T(8,128)(2,1)S(1)} %copy-done), kind=kOutput, calls=%fused_computation.1 | convolution fusion | flops 2416312320 | bytes 3407872 | tf_op jit(solution)/shard_map/dot_general | solution.py:156
  (71 shorter events, 7.9 us)
Async XLA Ops:
  7.2 1.2 copy-start
  7.2 3.9 %copy-start.4 = (u32[32]{0:T(128)S(1)}, u32[32]{0:T(128)}, u32[]{:S(2)}) copy-start(u32[32]{0:T(128)} %constant.91) | copy-start | bytes 388
  7.2 50.6 %all-reduce.4.cloned.1.call-start = ((), (), s32[]{:S(2)}) async-start(), calls=%async_computation.5 | async-start | bytes 1572864
  11.0 49.2 %copy-start.2 = (f32[128,256]{1,0:T(8,128)S(1)}, f32[128,256]{1,0:T(8,128)}, u32[]{:S(2)}) copy-start(f32[128,256]{1,0:T(8,128)} %param.8) | copy-start | bytes 393220
  11.0 49.4 %copy-start.3 = (s32[128]{0:T(128)S(1)}, s32[128]{0:T(128)}, u32[]{:S(2)}) copy-start(s32[128]{0:T(128)} %param.5) | copy-start | bytes 1540
  11.0 74.2 %all-gather.3.cloned.1.call-start = ((), (), s32[]{:S(2)}) async-start(), calls=%async_computation.3 | async-start | bytes 1769472 | tf_op jit(solution)/shard_map/all_gather | solution.py:115
  89.9 3.2 %copy-start.1 = (f32[128,256]{1,0:T(8,128)S(1)}, f32[128,256]{1,0:T(8,128)}, u32[]{:S(2)}) copy-start(f32[128,256]{1,0:T(8,128)} %param.9) | copy-start | bytes 393220
  94.6 13.2 %all-to-all-start = ((f32[128,3,256]{0,1,2:T(4,128)}), f32[128,3,256]{0,1,2:T(4,128)S(1)}, u32[]{:S(2)}, u32[]{:S(2)}) async-start(f32[128,3,256]{0,1,2:T(4,128)} %copy.147), calls=%async_computation | async-start | bytes 1048576 | tf_op jit(solution)/shard_map/all_to_all | solution.py:124
  98.1 87.2 %reduce-scatter.5.cloned.1.call-start = ((), (), s32[]{:S(2)}) async-start(), calls=%async_computation.4 | async-start | bytes 1769472 | tf_op jit(solution)/shard_map/reduce_scatter | solution.py:151
Sparse Core Ops, SparseCore 0:
  11.2 46.5 all-reduce.3
  60.4 24.8 all-gather.2
  147.9 37.3 reduce-scatter.4
